TPU v7x, 512 devices: a whole 4x4x16 slice. The times are simulated.
512 devices in a mesh: group: 8 (over y, x_lo), member: 64 (over z, x_hi, core).
Axes of the slice: x: 4 (x_hi: 2, x_lo: 2; x = x_hi * 2 + x_lo), y: 4, z: 16, core: 2. Of those that a mesh axis runs over, the one named last changes fastest.
Arguments:
- student: bfloat16 [196608, 768], P(('group', 'member')), may hold values from -0.29882812 to 0.29882812
- teacher: bfloat16 [196608, 1024], P(('group', 'member')), may hold values from -14 to 14
- counts: int32 [196608], P(('group', 'member')), may hold values from 1 to 7, as said below
- plan: int32 [8, 64, 5], P('group', 'member'), may hold values from 0 to 1, as said below
Outputs:
- grad_student: float32 [196608, 768], P(('group', 'member'))
- loss: float32 [], replicated
Inputs may be any that keep to these rules, and one draw needn't show every extreme that they name: `counts`: each row's count is a whole number from 1 up. The pairing is symmetric: plan[g, m, 2 + k - 1] equals plan[g, (m + k) mod 64, k - 1] for k = 1 to 2, and plan[g, m, 4] equals plan[g xor 1, m, 4].
All inputs are finite; a program needn't handle non-finite values.
Results may differ from a plain program's by a relative error of at most 0.0046.
Values may be sent and summed in bfloat16 or wider, within the bound.
A program may use at most 64 MiB of HBM per device.

v0:
```python
import jax
import jax.numpy as jnp
from jax import lax
from jax.sharding import PartitionSpec as P

EPS = 1e-06


def passed_along(value, axis, steps):
    count = lax.axis_size(axis)
    pairs = [(source, (source + steps) % count) for source in range(count)]
    return lax.ppermute(value, axis, pairs)


def partner_2(block, axis, bit):
    count = lax.axis_size(axis)
    route = []
    for low in range(count):
        high = low | 1 << bit
        if high != low and high < count:
            route += [(low, high), (high, low)]
    return lax.ppermute(block, axis, route)


def normalize(embeddings):
    widened = embeddings.astype(jnp.float32)
    row_scale = lax.rsqrt(jnp.sum(widened * widened, axis=-1, keepdims=True) + EPS)
    return ((widened * row_scale).astype(jnp.bfloat16), row_scale)


def block_terms(local_rows, partner, switch):
    local_s, local_t, local_w = local_rows
    partner_s, partner_t, partner_w = partner
    local_count = local_s.shape[0]
    features = local_s.shape[1]

    def compute(operand):
        student_sim = jnp.einsum(
            "id,jd->ij", local_s, partner_s, preferred_element_type=jnp.float32
        )
        teacher_sim = jnp.einsum(
            "id,jd->ij", local_t, partner_t, preferred_element_type=jnp.float32
        )
        mismatch = student_sim - teacher_sim
        pair_weight = local_w[:, None] * partner_w.astype(jnp.float32)[None, :]
        coefficient = (pair_weight * mismatch).astype(jnp.bfloat16)
        contrib = jnp.dot(coefficient, partner_s, preferred_element_type=jnp.float32)
        results = (contrib, jnp.sum(pair_weight * mismatch * mismatch), jnp.sum(pair_weight))
        return results

    def skipped(operand):
        results = (
            jnp.zeros((local_count, features), jnp.float32),
            jnp.float32(0.0),
            jnp.float32(0.0),
        )
        return results

    return lax.cond(switch > 0, compute, skipped, 0)


def per_device(student, teacher, counts, plan):
    unit_student, row_scale = normalize(student)
    unit_teacher, unused_scale = normalize(teacher)
    weights = counts.astype(jnp.float32)
    switches = plan.reshape(-1).astype(jnp.float32)
    span_blocks = (switches.shape[0] - 1) // 2
    local_rows = (unit_student, unit_teacher, weights)
    outgoing = (unit_student, unit_teacher, weights.astype(jnp.bfloat16))
    summed_grad, loss_sum, weight_sum = block_terms(local_rows, outgoing, jnp.float32(1.0))
    for offset in range(1, span_blocks + 1):
        lower = passed_along((outgoing[0], outgoing[1], outgoing[2]), "member", offset)
        upper = passed_along((outgoing[0], outgoing[1], outgoing[2]), "member", -offset)
        for column, partner in ((offset - 1, lower), (span_blocks + offset - 1, upper)):
            contrib, loss_part, weight_part = block_terms(local_rows, partner, switches[column])
            summed_grad = summed_grad + contrib
            loss_sum = loss_sum + loss_part
            weight_sum = weight_sum + weight_part
    partner = partner_2((outgoing[0], outgoing[1], outgoing[2]), "group", 0)
    contrib, loss_part, weight_part = block_terms(local_rows, partner, switches[2 * span_blocks])
    summed_grad = summed_grad + contrib
    loss_sum = loss_sum + loss_part
    weight_sum = weight_sum + weight_part
    loss_sum, weight_sum = lax.psum((loss_sum, weight_sum), ("group", "member"))
    unit_float = unit_student.astype(jnp.float32)
    along_unit = jnp.sum(summed_grad * unit_float, axis=-1, keepdims=True)
    grad_student = 4.0 * row_scale * (summed_grad - along_unit * unit_float)
    loss = student.shape[1] * loss_sum / weight_sum
    return (grad_student, loss)


def solution(mesh):
    return jax.shard_map(
        per_device,
        mesh=mesh,
        in_specs=(
            P(("group", "member"), None),
            P(("group", "member"), None),
            P(("group", "member")),
            P("group", "member", None),
        ),
        out_specs=(P(("group", "member"), None), P()),
        check_vma=False,
    )
```

profile of v0, /device:TPU:1, one launch (start us, length us, event | category | flops | bytes accessed | tf_op | source)
XLA Modules:
  0.0 263.8 jit_solution(1487551678774136010)
XLA Ops:
  0.7 1.5 fusion.35
  2.1 0.2 fusion.36
  2.3 0.0 copy-start.14
  2.4 6.0 %collective-permute-start.2 = (bf16[384,1024]{1,0:T(8,128)(2,1)S(1)}, bf16[384,1024]{1,0:T(8,128)(2,1)S(1)}, u32[]{:S(2)}, u32[]{:S(2)}) collective-permute-start(bf16[384,1024]{1,0:T(8,128)(2,1)S(1)} %fusion.36), channel_id=1, source_target_pairs={{0,1},{1,2},{2,3},{3,4},{4,5},{5,6},{6,7},{7,8},{8,9},{9,10},{10,1... | collective-permute-start | bytes 2359304 | tf_op jit(solution)/shard_map/ppermute | solution.py:12
  8.4 4.7 %collective-permute-start.5 = (bf16[384,1024]{1,0:T(8,128)(2,1)S(1)}, bf16[384,1024]{1,0:T(8,128)(2,1)S(1)}, u32[]{:S(2)}, u32[]{:S(2)}) collective-permute-start(bf16[384,1024]{1,0:T(8,128)(2,1)S(1)} %fusion.36), channel_id=1, source_target_pairs={{0,63},{1,0},{2,1},{3,2},{4,3},{5,4},{6,5},{7,6},{8,7},{9,8},{10,9... | collective-permute-start | bytes 2359304 | tf_op jit(solution)/shard_map/ppermute | solution.py:12
  13.1 2.4 collective-permute-start
  15.5 7.4 %collective-permute-start.3 = (bf16[384]{0:T(512)(128)(2,1)S(1)}, bf16[384]{0:T(512)(128)(2,1)S(1)}, u32[]{:S(2)}, u32[]{:S(2)}) collective-permute-start(bf16[384]{0:T(512)(128)(2,1)S(1)} %get-tuple-element.139), channel_id=1, source_target_pairs={{0,63},{1,0},{2,1},{3,2},{4,3},{5,4},{6,5},{7,6},{8,7},{9,8},{10,9... | collective-permute-start | bytes 2312 | tf_op jit(solution)/shard_map/ppermute | solution.py:12
  23.0 1.9 collective-permute-start.6
  24.9 0.2 fusion.37
  25.1 0.2 fusion.38
  25.3 0.5 collective-permute-done
  25.8 5.9 %collective-permute-start.1 = (bf16[384,768]{1,0:T(8,128)(2,1)S(1)}, bf16[384,768]{1,0:T(8,128)(2,1)S(1)}, u32[]{:S(2)}, u32[]{:S(2)}) collective-permute-start(bf16[384,768]{1,0:T(8,128)(2,1)S(1)} %fusion.38), channel_id=1, source_target_pairs={{0,1},{1,2},{2,3},{3,4},{4,5},{5,6},{6,7},{7,8},{8,9},{9,10},{10,1... | collective-permute-start | bytes 1769480 | tf_op jit(solution)/shard_map/ppermute | solution.py:12
  31.7 0.0 collective-permute-done.3
  31.7 7.7 %collective-permute-start.9 = (bf16[384]{0:T(512)(128)(2,1)S(1)}, bf16[384]{0:T(512)(128)(2,1)S(1)}, u32[]{:S(2)}, u32[]{:S(2)}) collective-permute-start(bf16[384]{0:T(512)(128)(2,1)S(1)} %get-tuple-element.139), channel_id=1, source_target_pairs={{0,62},{1,63},{2,0},{3,1},{4,2},{5,3},{6,4},{7,5},{8,6},{9,7},{10,... | collective-permute-start | bytes 2312 | tf_op jit(solution)/shard_map/ppermute | solution.py:12
  39.5 0.0 collective-permute-done.6
  39.5 5.4 %collective-permute-start.4 = (bf16[384,768]{1,0:T(8,128)(2,1)S(1)}, bf16[384,768]{1,0:T(8,128)(2,1)S(1)}, u32[]{:S(2)}, u32[]{:S(2)}) collective-permute-start(bf16[384,768]{1,0:T(8,128)(2,1)S(1)} %fusion.38), channel_id=1, source_target_pairs={{0,63},{1,0},{2,1},{3,2},{4,3},{5,4},{6,5},{7,6},{8,7},{9,8},{10,9... | collective-permute-start | bytes 1769480 | tf_op jit(solution)/shard_map/ppermute | solution.py:12
  44.9 0.0 collective-permute-done.9
  44.9 1.9 collective-permute-start.7
  46.8 0.0 collective-permute-done.1
  46.9 1.9 collective-permute-start.8
  48.8 3.4 %collective-permute-done.4 = bf16[384,768]{1,0:T(8,128)(2,1)S(1)} collective-permute-done((bf16[384,768]{1,0:T(8,128)(2,1)S(1)}, bf16[384,768]{1,0:T(8,128)(2,1)S(1)}, u32[]{:S(2)}, u32[]{:S(2)}) %collective-permute-start.4) | collective-permute-done | bytes 589856 | tf_op jit(solution)/shard_map/ppermute | solution.py:12
  52.2 10.2 %collective-permute-start.11 = (bf16[384,1024]{1,0:T(8,128)(2,1)S(1)}, bf16[384,1024]{1,0:T(8,128)(2,1)}, u32[]{:S(2)}, u32[]{:S(2)}) collective-permute-start(bf16[384,1024]{1,0:T(8,128)(2,1)S(1)} %fusion.36), channel_id=1, source_target_pairs={{0,62},{1,63},{2,0},{3,1},{4,2},{5,3},{6,4},{7,5},{8,6},{9,7},{10,... | collective-permute-start | bytes 2359304 | tf_op jit(solution)/shard_map/ppermute | solution.py:12
  62.4 2.7 %collective-permute-done.7 = bf16[384,768]{1,0:T(8,128)(2,1)S(1)} collective-permute-done((bf16[384,768]{1,0:T(8,128)(2,1)S(1)}, bf16[384,768]{1,0:T(8,128)(2,1)S(1)}, u32[]{:S(2)}, u32[]{:S(2)}) %collective-permute-start.7) | collective-permute-done | bytes 589856 | tf_op jit(solution)/shard_map/ppermute | solution.py:12
  65.0 0.8 copy-done.5
  65.9 2.2 collective-permute-start.14
  68.1 0.0 collective-permute-done.2
  68.1 27.2 %collective-permute-start.10 = (bf16[384,768]{1,0:T(8,128)(2,1)S(1)}, bf16[384,768]{1,0:T(8,128)(2,1)}, u32[]{:S(2)}, u32[]{:S(2)}) collective-permute-start(bf16[384,768]{1,0:T(8,128)(2,1)S(1)} %fusion.38), channel_id=1, source_target_pairs={{0,62},{1,63},{2,0},{3,1},{4,2},{5,3},{6,4},{7,5},{8,6},{9,7},{10,... | collective-permute-start | bytes 1769480 | tf_op jit(solution)/shard_map/ppermute | solution.py:12
  95.3 0.0 collective-permute-done.5
  95.3 0.0 copy-start.11
  95.3 1.9 collective-permute-start.13
  97.2 0.7 fusion.50
  101.1 0.6 fusion.56
  101.7 2.0 multiply_reduce_fusion.5
  103.7 5.4 %conditional.5 = (f32[384,768]{1,0:T(8,128)S(1)}, f32[]{:T(128)}, f32[]{:T(128)}) conditional(s32[]{:T(128)} %bitcast, () %tuple.48, (f32[384]{0:T(512)S(1)}, bf16[384]{0:T(512)(128)(2,1)S(1)}, bf16[384,768]{1,0:T(8,128)(2,1)S(1)}, bf16[384,768]{1,0:T(8,128)(2,1)}, bf16[384,1024]{1,0:T(8,128)(2,1)S(1)}, ...), branch_computations={%region_2.0_spmd, %region_3.6_spmd} | conditional | flops 756302208 | bytes 12394840 | solution.py:59
  103.7 0.9 copy-done.12
  104.6 1.7 fusion.51
  106.3 1.1 multiply_reduce_fusion
  107.4 0.5 fusion.3
  109.7 0.0 collective-permute-done.8
  109.8 3.4 %collective-permute-start.12 = (bf16[384]{0:T(512)(128)(2,1)S(1)}, bf16[384]{0:T(512)(128)(2,1)S(1)}, u32[]{:S(2)}, u32[]{:S(2)}) collective-permute-start(bf16[384]{0:T(512)(128)(2,1)S(1)} %get-tuple-element.139), channel_id=1, source_target_pairs={{0,64},{64,0},{128,192},{192,128},{256,320},{320,256},{384,448},{4... | collective-permute-start | bytes 2312 | tf_op jit(solution)/shard_map/ppermute | solution.py:22
  113.1 5.9 %conditional.6 = (f32[384,768]{1,0:T(8,128)}, f32[]{:T(128)}, f32[]{:T(128)}) conditional(s32[]{:T(128)} %bitcast.1, () %tuple.50, (f32[384]{0:T(512)S(1)}, bf16[384]{0:T(512)(128)(2,1)S(1)}, bf16[384,768]{1,0:T(8,128)(2,1)S(1)}, bf16[384,768]{1,0:T(8,128)(2,1)}, bf16[384,1024]{1,0:T(8,128)(2,1)S(1)}, /*index=5*/bf16[384,1024]{1,0:T(8,128)(2,1)}) %tuple.92), branch_computations={%region_6.7_spmd, %region_7.10_spmd} | conditional | flops 756302208 | bytes 9249084 | solution.py:59
  113.2 1.8 fusion.52
  115.0 1.2 multiply_reduce_fusion.1
  116.1 1.6 fusion.10
  119.0 4.7 %conditional.7 = (f32[384,768]{1,0:T(8,128)S(1)}, f32[]{:T(128)}, f32[]{:T(128)}) conditional(s32[]{:T(128)} %bitcast.2, () %tuple.52, (f32[384]{0:T(512)S(1)}, bf16[384]{0:T(512)(128)(2,1)S(1)}, bf16[384,768]{1,0:T(8,128)(2,1)S(1)}, bf16[384,768]{1,0:T(8,128)(2,1)}, bf16[384,1024]{1,0:T(8,128)(2,1)S(1)}, ...), branch_computations={%region_10.11_spmd, %region_11.14_spmd} | conditional | flops 756302208 | bytes 9249084 | solution.py:59
  119.1 1.8 fusion.53
  120.9 1.2 multiply_reduce_fusion.2
  122.0 0.5 fusion.17
  123.8 5.2 %collective-permute-done.10 = bf16[384,768]{1,0:T(8,128)(2,1)} collective-permute-done((bf16[384,768]{1,0:T(8,128)(2,1)S(1)}, bf16[384,768]{1,0:T(8,128)(2,1)}, u32[]{:S(2)}, u32[]{:S(2)}) %collective-permute-start.10) | collective-permute-done | bytes 589856 | tf_op jit(solution)/shard_map/ppermute | solution.py:12
  129.0 0.0 collective-permute-done.11
  129.0 7.9 %conditional.8 = (f32[384,768]{1,0:T(8,128)}, f32[]{:T(128)}, f32[]{:T(128)}) conditional(s32[]{:T(128)} %bitcast.3, () %tuple.54, (f32[384]{0:T(512)S(1)}, bf16[384]{0:T(512)(128)(2,1)S(1)}, bf16[384,768]{1,0:T(8,128)(2,1)S(1)}, bf16[384,768]{1,0:T(8,128)(2,1)}, bf16[384,1024]{1,0:T(8,128)(2,1)S(1)}, /*index=5*/bf16[384,1024]{1,0:T(8,128)(2,1)}) %tuple.55), branch_computations={%region_14.15_spmd, %region_15.18_spmd} | conditional | flops 756302208 | bytes 6889760 | solution.py:59
  129.0 1.7 fusion.54
  130.7 2.3 multiply_reduce_fusion.3
  133.0 2.6 fusion.24
  136.9 0.0 collective-permute-done.12
  136.9 0.0 collective-permute-done.13
  137.0 0.1 conditional.9
  137.0 0.1 broadcast.47
  137.1 0.0 copy-start.3
  137.8 0.3 copy-done.3
  138.1 1.6 fusion.45
  139.7 117.2 %all-reduce = (f32[]{:T(128)}, f32[]{:T(128)}) all-reduce(f32[]{:T(128)S(6)} %add.79, f32[]{:T(128)S(6)} %add.84), channel_id=1, replica_groups=mesh['group'=8,'member'=64] {'group','member'}, use_global_device_ids=true, to_apply=%region_24.0 | all-reduce | flops 2 | bytes 16 | tf_op jit(solution)/shard_map/psum | solution.py:84
  258.2 3.2 %fusion.39 = (f32[384]{0:T(512)S(1)}, f32[384,768]{1,0:T(8,128)S(1)}) fusion(f32[384,768]{1,0:T(8,128)} %copy-done.3, f32[384,768]{1,0:T(8,128)} %get-tuple-element.110, f32[384,768]{1,0:T(8,128)} %copy-done.2, f32[384,768]{1,0:T(8,128)} %get-tuple-element.108, f32[384,768]{1,0:T(8,128)S(1)} %fusion.45, f32[384,768]{1,0:T(8,128)} %copy-done.1, ...), kind=kLoop, calls=%fused_computation.56 | loop fusion | flops 3243648 | bytes 8850432 | tf_op jit(solution)/shard_map/reduce_sum | solution.py:86
  261.4 1.3 fusion.41
  (33 shorter events, 0.1 us)
Async XLA Ops:
  0.6 1.5 copy-start.4
  0.6 12.4 %copy-start.13 = (s32[384]{0:T(512)S(1)}, s32[384]{0:T(512)}, u32[]{:S(2)}) copy-start(s32[384]{0:T(512)} %param.16) | copy-start | bytes 4612
  0.6 24.2 %copy-start = (bf16[384,768]{1,0:T(8,128)(2,1)S(1)}, bf16[384,768]{1,0:T(8,128)(2,1)}, u32[]{:S(2)}) copy-start(bf16[384,768]{1,0:T(8,128)(2,1)} %param.14) | copy-start | bytes 1769476
  2.3 65.8 %copy-start.14 = (s32[1,1,5]{2,1,0:T(1,128)S(1)}, s32[1,1,5]{2,1,0:T(1,128)}, u32[]{:S(2)}) copy-start(s32[1,1,5]{2,1,0:T(1,128)} %param.17) | copy-start | bytes 64
  2.4 65.8 %collective-permute-start.2 = (bf16[384,1024]{1,0:T(8,128)(2,1)S(1)}, bf16[384,1024]{1,0:T(8,128)(2,1)S(1)}, u32[]{:S(2)}, u32[]{:S(2)}) collective-permute-start(bf16[384,1024]{1,0:T(8,128)(2,1)S(1)} %fusion.36), channel_id=1, source_target_pairs={{0,1},{1,2},{2,3},{3,4},{4,5},{5,6},{6,7},{7,8},{8,9},{9,10},{10,1... | collective-permute-start | bytes 2359304 | tf_op jit(solution)/shard_map/ppermute | solution.py:12
  8.4 86.9 %collective-permute-start.5 = (bf16[384,1024]{1,0:T(8,128)(2,1)S(1)}, bf16[384,1024]{1,0:T(8,128)(2,1)S(1)}, u32[]{:S(2)}, u32[]{:S(2)}) collective-permute-start(bf16[384,1024]{1,0:T(8,128)(2,1)S(1)} %fusion.36), channel_id=1, source_target_pairs={{0,63},{1,0},{2,1},{3,2},{4,3},{5,4},{6,5},{7,6},{8,7},{9,8},{10,9... | collective-permute-start | bytes 2359304 | tf_op jit(solution)/shard_map/ppermute | solution.py:12
  13.1 12.7 %collective-permute-start = (bf16[384]{0:T(512)(128)(2,1)S(1)}, bf16[384]{0:T(512)(128)(2,1)S(1)}, u32[]{:S(2)}, u32[]{:S(2)}) collective-permute-start(bf16[384]{0:T(512)(128)(2,1)S(1)} %get-tuple-element.139), channel_id=1, source_target_pairs={{0,1},{1,2},{2,3},{3,4},{4,5},{5,6},{6,7},{7,8},{8,9},{9,10},{10,1... | collective-permute-start | bytes 2312 | tf_op jit(solution)/shard_map/ppermute | solution.py:12
  15.5 16.2 %collective-permute-start.3 = (bf16[384]{0:T(512)(128)(2,1)S(1)}, bf16[384]{0:T(512)(128)(2,1)S(1)}, u32[]{:S(2)}, u32[]{:S(2)}) collective-permute-start(bf16[384]{0:T(512)(128)(2,1)S(1)} %get-tuple-element.139), channel_id=1, source_target_pairs={{0,63},{1,0},{2,1},{3,2},{4,3},{5,4},{6,5},{7,6},{8,7},{9,8},{10,9... | collective-permute-start | bytes 2312 | tf_op jit(solution)/shard_map/ppermute | solution.py:12
  23.0 16.5 %collective-permute-start.6 = (bf16[384]{0:T(512)(128)(2,1)S(1)}, bf16[384]{0:T(512)(128)(2,1)S(1)}, u32[]{:S(2)}, u32[]{:S(2)}) collective-permute-start(bf16[384]{0:T(512)(128)(2,1)S(1)} %get-tuple-element.139), channel_id=1, source_target_pairs={{0,2},{1,3},{2,4},{3,5},{4,6},{5,7},{6,8},{7,9},{8,10},{9,11},{10,... | collective-permute-start | bytes 2312 | tf_op jit(solution)/shard_map/ppermute | solution.py:12
  25.8 21.1 %collective-permute-start.1 = (bf16[384,768]{1,0:T(8,128)(2,1)S(1)}, bf16[384,768]{1,0:T(8,128)(2,1)S(1)}, u32[]{:S(2)}, u32[]{:S(2)}) collective-permute-start(bf16[384,768]{1,0:T(8,128)(2,1)S(1)} %fusion.38), channel_id=1, source_target_pairs={{0,1},{1,2},{2,3},{3,4},{4,5},{5,6},{6,7},{7,8},{8,9},{9,10},{10,1... | collective-permute-start | bytes 1769480 | tf_op jit(solution)/shard_map/ppermute | solution.py:12
  31.7 13.2 %collective-permute-start.9 = (bf16[384]{0:T(512)(128)(2,1)S(1)}, bf16[384]{0:T(512)(128)(2,1)S(1)}, u32[]{:S(2)}, u32[]{:S(2)}) collective-permute-start(bf16[384]{0:T(512)(128)(2,1)S(1)} %get-tuple-element.139), channel_id=1, source_target_pairs={{0,62},{1,63},{2,0},{3,1},{4,2},{5,3},{6,4},{7,5},{8,6},{9,7},{10,... | collective-permute-start | bytes 2312 | tf_op jit(solution)/shard_map/ppermute | solution.py:12
  39.5 12.7 %collective-permute-start.4 = (bf16[384,768]{1,0:T(8,128)(2,1)S(1)}, bf16[384,768]{1,0:T(8,128)(2,1)S(1)}, u32[]{:S(2)}, u32[]{:S(2)}) collective-permute-start(bf16[384,768]{1,0:T(8,128)(2,1)S(1)} %fusion.38), channel_id=1, source_target_pairs={{0,63},{1,0},{2,1},{3,2},{4,3},{5,4},{6,5},{7,6},{8,7},{9,8},{10,9... | collective-permute-start | bytes 1769480 | tf_op jit(solution)/shard_map/ppermute | solution.py:12
  44.9 20.1 %collective-permute-start.7 = (bf16[384,768]{1,0:T(8,128)(2,1)S(1)}, bf16[384,768]{1,0:T(8,128)(2,1)S(1)}, u32[]{:S(2)}, u32[]{:S(2)}) collective-permute-start(bf16[384,768]{1,0:T(8,128)(2,1)S(1)} %fusion.38), channel_id=1, source_target_pairs={{0,2},{1,3},{2,4},{3,5},{4,6},{5,7},{6,8},{7,9},{8,10},{9,11},{10,... | collective-permute-start | bytes 1769480 | tf_op jit(solution)/shard_map/ppermute | solution.py:12
  46.8 18.2 %copy-start.9 = (bf16[384,768]{1,0:T(8,128)(2,1)}, bf16[384,768]{1,0:T(8,128)(2,1)S(1)}, u32[]{:S(2)}) copy-start(bf16[384,768]{1,0:T(8,128)(2,1)S(1)} %collective-permute-done.1) | copy-start | bytes 1769476
  46.9 62.9 %collective-permute-start.8 = (bf16[384,1024]{1,0:T(8,128)(2,1)S(1)}, bf16[384,1024]{1,0:T(8,128)(2,1)}, u32[]{:S(2)}, u32[]{:S(2)}) collective-permute-start(bf16[384,1024]{1,0:T(8,128)(2,1)S(1)} %fusion.36), channel_id=1, source_target_pairs={{0,2},{1,3},{2,4},{3,5},{4,6},{5,7},{6,8},{7,9},{8,10},{9,11},{10,... | collective-permute-start | bytes 2359304 | tf_op jit(solution)/shard_map/ppermute | solution.py:12
  52.2 12.9 %copy-start.7 = (bf16[384,768]{1,0:T(8,128)(2,1)}, bf16[384,768]{1,0:T(8,128)(2,1)S(1)}, u32[]{:S(2)}) copy-start(bf16[384,768]{1,0:T(8,128)(2,1)S(1)} %collective-permute-done.4) | copy-start | bytes 1769476
  52.2 76.8 %collective-permute-start.11 = (bf16[384,1024]{1,0:T(8,128)(2,1)S(1)}, bf16[384,1024]{1,0:T(8,128)(2,1)}, u32[]{:S(2)}, u32[]{:S(2)}) collective-permute-start(bf16[384,1024]{1,0:T(8,128)(2,1)S(1)} %fusion.36), channel_id=1, source_target_pairs={{0,62},{1,63},{2,0},{3,1},{4,2},{5,3},{6,4},{7,5},{8,6},{9,7},{10,... | collective-permute-start | bytes 2359304 | tf_op jit(solution)/shard_map/ppermute | solution.py:12
  65.0 0.8 copy-start.5
  65.9 71.1 %collective-permute-start.14 = (bf16[384,1024]{1,0:T(8,128)(2,1)S(1)}, bf16[384,1024]{1,0:T(8,128)(2,1)}, u32[]{:S(2)}, u32[]{:S(2)}) collective-permute-start(bf16[384,1024]{1,0:T(8,128)(2,1)S(1)} %fusion.36), channel_id=1, source_target_pairs={{0,64},{64,0},{128,192},{192,128},{256,320},{320,256},{384,448},{4... | collective-permute-start | bytes 2359304 | tf_op jit(solution)/shard_map/ppermute | solution.py:22
  68.1 60.8 %collective-permute-start.10 = (bf16[384,768]{1,0:T(8,128)(2,1)S(1)}, bf16[384,768]{1,0:T(8,128)(2,1)}, u32[]{:S(2)}, u32[]{:S(2)}) collective-permute-start(bf16[384,768]{1,0:T(8,128)(2,1)S(1)} %fusion.38), channel_id=1, source_target_pairs={{0,62},{1,63},{2,0},{3,1},{4,2},{5,3},{6,4},{7,5},{8,6},{9,7},{10,... | collective-permute-start | bytes 1769480 | tf_op jit(solution)/shard_map/ppermute | solution.py:12
  95.3 5.8 %copy-start.11 = (bf16[384,1024]{1,0:T(8,128)(2,1)}, bf16[384,1024]{1,0:T(8,128)(2,1)S(1)}, u32[]{:S(2)}) copy-start(bf16[384,1024]{1,0:T(8,128)(2,1)S(1)} %collective-permute-done.5) | copy-start | bytes 2359300
  95.3 41.6 %collective-permute-start.13 = (bf16[384,768]{1,0:T(8,128)(2,1)S(1)}, bf16[384,768]{1,0:T(8,128)(2,1)}, u32[]{:S(2)}, u32[]{:S(2)}) collective-permute-start(bf16[384,768]{1,0:T(8,128)(2,1)S(1)} %fusion.38), channel_id=1, source_target_pairs={{0,64},{64,0},{128,192},{192,128},{256,320},{320,256},{384,448},{4... | collective-permute-start | bytes 1769480 | tf_op jit(solution)/shard_map/ppermute | solution.py:22
  103.7 0.9 copy-start.12
  103.7 2.6 copy-start.10
  109.1 4.0 %copy-start.1 = (f32[384,768]{1,0:T(8,128)}, f32[384,768]{1,0:T(8,128)S(1)}, u32[]{:S(2)}) copy-start(f32[384,768]{1,0:T(8,128)S(1)} %get-tuple-element.107) | copy-start | bytes 3538948
  109.8 27.2 %collective-permute-start.12 = (bf16[384]{0:T(512)(128)(2,1)S(1)}, bf16[384]{0:T(512)(128)(2,1)S(1)}, u32[]{:S(2)}, u32[]{:S(2)}) collective-permute-start(bf16[384]{0:T(512)(128)(2,1)S(1)} %get-tuple-element.139), channel_id=1, source_target_pairs={{0,64},{64,0},{128,192},{192,128},{256,320},{320,256},{384,448},{4... | collective-permute-start | bytes 2312 | tf_op jit(solution)/shard_map/ppermute | solution.py:22
  113.2 1.8 copy-start.8
  119.0 1.8 copy-start.6
  123.8 5.2 %copy-start.2 = (f32[384,768]{1,0:T(8,128)}, f32[384,768]{1,0:T(8,128)S(1)}, u32[]{:S(2)}) copy-start(f32[384,768]{1,0:T(8,128)S(1)} %get-tuple-element.109) | copy-start | bytes 3538948
  137.1 1.0 copy-start.3
where the time goes:
time: 265 us; the launch traced here: 264 us
  blocking collectives  117 us (44%)
  starting transfers between devices  90.2 us (34%)
  matrix products  22 us (8%)
  waiting for transfers between devices  11.8 us (4%)
  between operations  7.98 us (3%)
  other arithmetic  6.54 us (2%)
  loops' own time  5.19 us (2%)
  local copies, waits for them, and re-layouts  2.83 us (1%)
    psum x1, blocking collectives, per_device(): loss_sum, weight_sum = lax.psum((loss_sum, weight_sum), ('group', 'member'))  117 us
    ppermute x12, starting transfers between devices, passed_along(): return lax.ppermute(value, axis, pairs)  82.7 us
    ppermute x12, waiting for transfers between devices, passed_along(): return lax.ppermute(value, axis, pairs)  11.8 us
    dot_general x5, matrix products, compute(): jnp.einsum('id,jd->ij', local_s, partner_s, preferred_element_type=jnp.fl...  7.7 us
    dot_general x5, matrix products, compute(): jnp.einsum('id,jd->ij', local_t, partner_t, preferred_element_type=jnp.fl...  7.59 us
    ppermute x3, starting transfers between devices, partner_2(): return lax.ppermute(block, axis, route)  7.5 us
    dot_general x5, matrix products, compute(): jnp.dot(coefficient, partner_s, preferred_element_type=jnp.float32)  6.75 us
  transfers between devices with their start and end apart: 15, of which 4 were waited for; matrix products, arithmetic and copies ran while one was open for 8% of the time, Pallas kernels for 0%

commit v1 on v0

--- a/solution.py
+++ b/solution.py
@@ -81,7 +81,7 @@
     summed_grad = summed_grad + contrib
     loss_sum = loss_sum + loss_part
     weight_sum = weight_sum + weight_part
-    loss_sum, weight_sum = lax.psum((loss_sum, weight_sum), ("group", "member"))
+    loss_sum, weight_sum = lax.psum(lax.psum((loss_sum, weight_sum), "group"), "member")
     unit_float = unit_student.astype(jnp.float32)
     along_unit = jnp.sum(summed_grad * unit_float, axis=-1, keepdims=True)
     grad_student = 4.0 * row_scale * (summed_grad - along_unit * unit_float)

time: 265 us -> 305 us (1.15)
  blocking collectives: 117 us -> 156 us
    psum x1 -> x2, blocking collectives: 117 us -> 156 us  [the longest x1 134 us: per_device(): lax.psum(lax.psum((loss_sum, weight_sum), 'group'), 'member')]
  transfers between devices with their start and end apart: 15 -> 15, of which waited for: 4 -> 4; matrix products, arithmetic and copies ran while one was open for 8% -> 7% of each run, Pallas kernels for 0% -> 0%
where the time goes in v1:
time: 305 us; the launch traced here: 303 us
  blocking collectives  156 us (51%)
  starting transfers between devices  90.2 us (30%)
  matrix products  22.1 us (7%)
  waiting for transfers between devices  11.8 us (4%)
  between operations  7.73 us (3%)
  other arithmetic  6.54 us (2%)
  loops' own time  5.3 us (2%)
    psum x1, blocking collectives, per_device(): lax.psum(lax.psum((loss_sum, weight_sum), 'group'), 'member')  134 us
    ppermute x12, starting transfers between devices, passed_along(): return lax.ppermute(value, axis, pairs)  82.7 us
    psum x1, blocking collectives, per_device(): lax.psum((loss_sum, weight_sum), 'group')  22.6 us
    ppermute x12, waiting for transfers between devices, passed_along(): return lax.ppermute(value, axis, pairs)  11.8 us
    dot_general x5, matrix products, compute(): jnp.einsum('id,jd->ij', local_s, partner_s, preferred_element_type=jnp.fl...  7.72 us
    dot_general x5, matrix products, compute(): jnp.einsum('id,jd->ij', local_t, partner_t, preferred_element_type=jnp.fl...  7.6 us
    ppermute x3, starting transfers between devices, partner_2(): return lax.ppermute(block, axis, route)  7.49 us
    dot_general x5, matrix products, compute(): jnp.dot(coefficient, partner_s, preferred_element_type=jnp.float32)  6.73 us
  transfers between devices with their start and end apart: 15, of which 4 were waited for; matrix products, arithmetic and copies ran while one was open for 7% of the time, Pallas kernels for 0%

profile of v1, /device:TPU:1, one launch (start us, length us, event | category | flops | bytes accessed | tf_op | source)
XLA Modules:
  0.0 303.0 jit_solution(12060177593051732516)
XLA Ops:
  0.7 1.5 fusion.35
  2.1 0.2 fusion.36
  2.3 0.0 copy-start.14
  2.4 6.0 %collective-permute-start.2 = (bf16[384,1024]{1,0:T(8,128)(2,1)S(1)}, bf16[384,1024]{1,0:T(8,128)(2,1)S(1)}, u32[]{:S(2)}, u32[]{:S(2)}) collective-permute-start(bf16[384,1024]{1,0:T(8,128)(2,1)S(1)} %fusion.36), channel_id=1, source_target_pairs={{0,1},{1,2},{2,3},{3,4},{4,5},{5,6},{6,7},{7,8},{8,9},{9,10},{10,1... | collective-permute-start | bytes 2359304 | tf_op jit(solution)/shard_map/ppermute | solution.py:12
  8.4 4.7 %collective-permute-start.5 = (bf16[384,1024]{1,0:T(8,128)(2,1)S(1)}, bf16[384,1024]{1,0:T(8,128)(2,1)S(1)}, u32[]{:S(2)}, u32[]{:S(2)}) collective-permute-start(bf16[384,1024]{1,0:T(8,128)(2,1)S(1)} %fusion.36), channel_id=1, source_target_pairs={{0,63},{1,0},{2,1},{3,2},{4,3},{5,4},{6,5},{7,6},{8,7},{9,8},{10,9... | collective-permute-start | bytes 2359304 | tf_op jit(solution)/shard_map/ppermute | solution.py:12
  13.1 2.4 collective-permute-start
  15.5 7.4 %collective-permute-start.3 = (bf16[384]{0:T(512)(128)(2,1)S(1)}, bf16[384]{0:T(512)(128)(2,1)S(1)}, u32[]{:S(2)}, u32[]{:S(2)}) collective-permute-start(bf16[384]{0:T(512)(128)(2,1)S(1)} %get-tuple-element.141), channel_id=1, source_target_pairs={{0,63},{1,0},{2,1},{3,2},{4,3},{5,4},{6,5},{7,6},{8,7},{9,8},{10,9... | collective-permute-start | bytes 2312 | tf_op jit(solution)/shard_map/ppermute | solution.py:12
  23.0 1.9 collective-permute-start.6
  24.9 0.2 fusion.37
  25.1 0.2 fusion.38
  25.3 0.5 collective-permute-done
  25.8 5.9 %collective-permute-start.1 = (bf16[384,768]{1,0:T(8,128)(2,1)S(1)}, bf16[384,768]{1,0:T(8,128)(2,1)S(1)}, u32[]{:S(2)}, u32[]{:S(2)}) collective-permute-start(bf16[384,768]{1,0:T(8,128)(2,1)S(1)} %fusion.38), channel_id=1, source_target_pairs={{0,1},{1,2},{2,3},{3,4},{4,5},{5,6},{6,7},{7,8},{8,9},{9,10},{10,1... | collective-permute-start | bytes 1769480 | tf_op jit(solution)/shard_map/ppermute | solution.py:12
  31.7 0.0 collective-permute-done.3
  31.7 7.7 %collective-permute-start.9 = (bf16[384]{0:T(512)(128)(2,1)S(1)}, bf16[384]{0:T(512)(128)(2,1)S(1)}, u32[]{:S(2)}, u32[]{:S(2)}) collective-permute-start(bf16[384]{0:T(512)(128)(2,1)S(1)} %get-tuple-element.141), channel_id=1, source_target_pairs={{0,62},{1,63},{2,0},{3,1},{4,2},{5,3},{6,4},{7,5},{8,6},{9,7},{10,... | collective-permute-start | bytes 2312 | tf_op jit(solution)/shard_map/ppermute | solution.py:12
  39.5 0.0 collective-permute-done.6
  39.5 5.4 %collective-permute-start.4 = (bf16[384,768]{1,0:T(8,128)(2,1)S(1)}, bf16[384,768]{1,0:T(8,128)(2,1)S(1)}, u32[]{:S(2)}, u32[]{:S(2)}) collective-permute-start(bf16[384,768]{1,0:T(8,128)(2,1)S(1)} %fusion.38), channel_id=1, source_target_pairs={{0,63},{1,0},{2,1},{3,2},{4,3},{5,4},{6,5},{7,6},{8,7},{9,8},{10,9... | collective-permute-start | bytes 1769480 | tf_op jit(solution)/shard_map/ppermute | solution.py:12
  44.9 0.0 collective-permute-done.9
  44.9 1.9 collective-permute-start.7
  46.8 0.0 collective-permute-done.1
  46.9 1.9 collective-permute-start.8
  48.8 3.4 %collective-permute-done.4 = bf16[384,768]{1,0:T(8,128)(2,1)S(1)} collective-permute-done((bf16[384,768]{1,0:T(8,128)(2,1)S(1)}, bf16[384,768]{1,0:T(8,128)(2,1)S(1)}, u32[]{:S(2)}, u32[]{:S(2)}) %collective-permute-start.4) | collective-permute-done | bytes 589856 | tf_op jit(solution)/shard_map/ppermute | solution.py:12
  52.2 10.2 %collective-permute-start.11 = (bf16[384,1024]{1,0:T(8,128)(2,1)S(1)}, bf16[384,1024]{1,0:T(8,128)(2,1)}, u32[]{:S(2)}, u32[]{:S(2)}) collective-permute-start(bf16[384,1024]{1,0:T(8,128)(2,1)S(1)} %fusion.36), channel_id=1, source_target_pairs={{0,62},{1,63},{2,0},{3,1},{4,2},{5,3},{6,4},{7,5},{8,6},{9,7},{10,... | collective-permute-start | bytes 2359304 | tf_op jit(solution)/shard_map/ppermute | solution.py:12
  62.4 2.7 collective-permute-done.7
  65.0 0.8 copy-done.5
  65.9 2.2 collective-permute-start.14
  68.1 0.0 collective-permute-done.2
  68.1 27.2 %collective-permute-start.10 = (bf16[384,768]{1,0:T(8,128)(2,1)S(1)}, bf16[384,768]{1,0:T(8,128)(2,1)}, u32[]{:S(2)}, u32[]{:S(2)}) collective-permute-start(bf16[384,768]{1,0:T(8,128)(2,1)S(1)} %fusion.38), channel_id=1, source_target_pairs={{0,62},{1,63},{2,0},{3,1},{4,2},{5,3},{6,4},{7,5},{8,6},{9,7},{10,... | collective-permute-start | bytes 1769480 | tf_op jit(solution)/shard_map/ppermute | solution.py:12
  95.3 0.0 collective-permute-done.5
  95.3 0.0 copy-start.11
  95.3 1.9 collective-permute-start.13
  97.2 0.7 fusion.50
  101.1 0.6 fusion.56
  101.7 1.9 multiply_reduce_fusion.5
  103.6 5.5 %conditional.5 = (f32[384,768]{1,0:T(8,128)S(1)}, f32[]{:T(128)}, f32[]{:T(128)}) conditional(s32[]{:T(128)} %bitcast, () %tuple.48, (f32[384]{0:T(512)S(1)}, bf16[384]{0:T(512)(128)(2,1)S(1)}, bf16[384,768]{1,0:T(8,128)(2,1)S(1)}, bf16[384,768]{1,0:T(8,128)(2,1)}, bf16[384,1024]{1,0:T(8,128)(2,1)S(1)}, ...), branch_computations={%region_2.0_spmd, %region_3.6_spmd} | conditional | flops 756302208 | bytes 12394840 | solution.py:59
  103.6 0.9 copy-done.12
  104.5 1.7 fusion.51
  106.2 1.1 multiply_reduce_fusion
  107.3 0.5 fusion.3
  109.7 0.0 collective-permute-done.8
  109.7 3.4 %collective-permute-start.12 = (bf16[384]{0:T(512)(128)(2,1)S(1)}, bf16[384]{0:T(512)(128)(2,1)S(1)}, u32[]{:S(2)}, u32[]{:S(2)}) collective-permute-start(bf16[384]{0:T(512)(128)(2,1)S(1)} %get-tuple-element.141), channel_id=1, source_target_pairs={{0,64},{64,0},{128,192},{192,128},{256,320},{320,256},{384,448},{4... | collective-permute-start | bytes 2312 | tf_op jit(solution)/shard_map/ppermute | solution.py:22
  113.1 5.9 %conditional.6 = (f32[384,768]{1,0:T(8,128)}, f32[]{:T(128)}, f32[]{:T(128)}) conditional(s32[]{:T(128)} %bitcast.1, () %tuple.50, (f32[384]{0:T(512)S(1)}, bf16[384]{0:T(512)(128)(2,1)S(1)}, bf16[384,768]{1,0:T(8,128)(2,1)S(1)}, bf16[384,768]{1,0:T(8,128)(2,1)}, bf16[384,1024]{1,0:T(8,128)(2,1)S(1)}, /*index=5*/bf16[384,1024]{1,0:T(8,128)(2,1)}) %tuple.92), branch_computations={%region_6.7_spmd, %region_7.10_spmd} | conditional | flops 756302208 | bytes 9249084 | solution.py:59
  113.1 1.8 fusion.52
  114.9 1.2 multiply_reduce_fusion.1
  116.1 1.5 fusion.10
  119.0 4.8 %conditional.7 = (f32[384,768]{1,0:T(8,128)S(1)}, f32[]{:T(128)}, f32[]{:T(128)}) conditional(s32[]{:T(128)} %bitcast.2, () %tuple.52, (f32[384]{0:T(512)S(1)}, bf16[384]{0:T(512)(128)(2,1)S(1)}, bf16[384,768]{1,0:T(8,128)(2,1)S(1)}, bf16[384,768]{1,0:T(8,128)(2,1)}, bf16[384,1024]{1,0:T(8,128)(2,1)S(1)}, ...), branch_computations={%region_10.11_spmd, %region_11.14_spmd} | conditional | flops 756302208 | bytes 9249084 | solution.py:59
  119.0 1.8 fusion.53
  120.8 1.2 multiply_reduce_fusion.2
  122.0 0.5 fusion.17
  123.8 5.2 %collective-permute-done.10 = bf16[384,768]{1,0:T(8,128)(2,1)} collective-permute-done((bf16[384,768]{1,0:T(8,128)(2,1)S(1)}, bf16[384,768]{1,0:T(8,128)(2,1)}, u32[]{:S(2)}, u32[]{:S(2)}) %collective-permute-start.10) | collective-permute-done | bytes 589856 | tf_op jit(solution)/shard_map/ppermute | solution.py:12
  129.0 7.9 %conditional.8 = (f32[384,768]{1,0:T(8,128)}, f32[]{:T(128)}, f32[]{:T(128)}) conditional(s32[]{:T(128)} %bitcast.3, () %tuple.54, (f32[384]{0:T(512)S(1)}, bf16[384]{0:T(512)(128)(2,1)S(1)}, bf16[384,768]{1,0:T(8,128)(2,1)S(1)}, bf16[384,768]{1,0:T(8,128)(2,1)}, bf16[384,1024]{1,0:T(8,128)(2,1)S(1)}, /*index=5*/bf16[384,1024]{1,0:T(8,128)(2,1)}) %tuple.55), branch_computations={%region_14.15_spmd, %region_15.18_spmd} | conditional | flops 756302208 | bytes 6889760 | solution.py:59
  129.0 1.7 fusion.54
  130.7 2.3 multiply_reduce_fusion.3
  133.0 2.6 fusion.24
  136.9 0.0 collective-permute-done.12
  136.9 0.0 collective-permute-done.14
  136.9 0.1 conditional.9
  137.0 0.1 broadcast.47
  137.1 0.0 copy-start.3
  137.7 0.4 copy-done.3
  138.1 1.6 fusion.45
  139.7 22.6 %all-reduce.1 = (f32[]{:T(128)}, f32[]{:T(128)}) all-reduce(f32[]{:T(128)S(6)} %add.83, f32[]{:T(128)S(6)} %add.88), channel_id=1, replica_groups=mesh['group'=8,'member'=64] {'group'}, use_global_device_ids=true, to_apply=%region_24.0 | all-reduce | flops 2 | bytes 16 | tf_op jit(solution)/shard_map/psum | solution.py:84
  162.2 133.9 %all-reduce = (f32[]{:T(128)}, f32[]{:T(128)}) all-reduce(f32[]{:T(128)} %get-tuple-element.136, f32[]{:T(128)} %get-tuple-element.137), channel_id=1, replica_groups=mesh['group'=8,'member'=64] {'member'}, use_global_device_ids=true, to_apply=%region_25.0 | all-reduce | flops 2 | bytes 16 | tf_op jit(solution)/shard_map/psum | solution.py:84
  297.4 3.2 %fusion.39 = (f32[384]{0:T(512)S(1)}, f32[384,768]{1,0:T(8,128)S(1)}) fusion(f32[384,768]{1,0:T(8,128)} %copy-done.3, f32[384,768]{1,0:T(8,128)} %get-tuple-element.110, f32[384,768]{1,0:T(8,128)} %copy-done.2, f32[384,768]{1,0:T(8,128)} %get-tuple-element.108, f32[384,768]{1,0:T(8,128)S(1)} %fusion.45, f32[384,768]{1,0:T(8,128)} %copy-done.1, ...), kind=kLoop, calls=%fused_computation.56 | loop fusion | flops 3243648 | bytes 8850432 | tf_op jit(solution)/shard_map/reduce_sum | solution.py:86
  300.6 1.3 fusion.41
  (34 shorter events, 0.1 us)
Async XLA Ops:
  0.6 1.5 copy-start.4
  0.6 12.4 %copy-start.13 = (s32[384]{0:T(512)S(1)}, s32[384]{0:T(512)}, u32[]{:S(2)}) copy-start(s32[384]{0:T(512)} %param.16) | copy-start | bytes 4612
  0.6 24.2 %copy-start = (bf16[384,768]{1,0:T(8,128)(2,1)S(1)}, bf16[384,768]{1,0:T(8,128)(2,1)}, u32[]{:S(2)}) copy-start(bf16[384,768]{1,0:T(8,128)(2,1)} %param.14) | copy-start | bytes 1769476
  2.3 65.7 %copy-start.14 = (s32[1,1,5]{2,1,0:T(1,128)S(1)}, s32[1,1,5]{2,1,0:T(1,128)}, u32[]{:S(2)}) copy-start(s32[1,1,5]{2,1,0:T(1,128)} %param.17) | copy-start | bytes 64
  2.4 65.8 %collective-permute-start.2 = (bf16[384,1024]{1,0:T(8,128)(2,1)S(1)}, bf16[384,1024]{1,0:T(8,128)(2,1)S(1)}, u32[]{:S(2)}, u32[]{:S(2)}) collective-permute-start(bf16[384,1024]{1,0:T(8,128)(2,1)S(1)} %fusion.36), channel_id=1, source_target_pairs={{0,1},{1,2},{2,3},{3,4},{4,5},{5,6},{6,7},{7,8},{8,9},{9,10},{10,1... | collective-permute-start | bytes 2359304 | tf_op jit(solution)/shard_map/ppermute | solution.py:12
  8.4 86.9 %collective-permute-start.5 = (bf16[384,1024]{1,0:T(8,128)(2,1)S(1)}, bf16[384,1024]{1,0:T(8,128)(2,1)S(1)}, u32[]{:S(2)}, u32[]{:S(2)}) collective-permute-start(bf16[384,1024]{1,0:T(8,128)(2,1)S(1)} %fusion.36), channel_id=1, source_target_pairs={{0,63},{1,0},{2,1},{3,2},{4,3},{5,4},{6,5},{7,6},{8,7},{9,8},{10,9... | collective-permute-start | bytes 2359304 | tf_op jit(solution)/shard_map/ppermute | solution.py:12
  13.1 12.7 %collective-permute-start = (bf16[384]{0:T(512)(128)(2,1)S(1)}, bf16[384]{0:T(512)(128)(2,1)S(1)}, u32[]{:S(2)}, u32[]{:S(2)}) collective-permute-start(bf16[384]{0:T(512)(128)(2,1)S(1)} %get-tuple-element.141), channel_id=1, source_target_pairs={{0,1},{1,2},{2,3},{3,4},{4,5},{5,6},{6,7},{7,8},{8,9},{9,10},{10,1... | collective-permute-start | bytes 2312 | tf_op jit(solution)/shard_map/ppermute | solution.py:12
  15.5 16.2 %collective-permute-start.3 = (bf16[384]{0:T(512)(128)(2,1)S(1)}, bf16[384]{0:T(512)(128)(2,1)S(1)}, u32[]{:S(2)}, u32[]{:S(2)}) collective-permute-start(bf16[384]{0:T(512)(128)(2,1)S(1)} %get-tuple-element.141), channel_id=1, source_target_pairs={{0,63},{1,0},{2,1},{3,2},{4,3},{5,4},{6,5},{7,6},{8,7},{9,8},{10,9... | collective-permute-start | bytes 2312 | tf_op jit(solution)/shard_map/ppermute | solution.py:12
  23.0 16.5 %collective-permute-start.6 = (bf16[384]{0:T(512)(128)(2,1)S(1)}, bf16[384]{0:T(512)(128)(2,1)S(1)}, u32[]{:S(2)}, u32[]{:S(2)}) collective-permute-start(bf16[384]{0:T(512)(128)(2,1)S(1)} %get-tuple-element.141), channel_id=1, source_target_pairs={{0,2},{1,3},{2,4},{3,5},{4,6},{5,7},{6,8},{7,9},{8,10},{9,11},{10,... | collective-permute-start | bytes 2312 | tf_op jit(solution)/shard_map/ppermute | solution.py:12
  25.8 21.1 %collective-permute-start.1 = (bf16[384,768]{1,0:T(8,128)(2,1)S(1)}, bf16[384,768]{1,0:T(8,128)(2,1)S(1)}, u32[]{:S(2)}, u32[]{:S(2)}) collective-permute-start(bf16[384,768]{1,0:T(8,128)(2,1)S(1)} %fusion.38), channel_id=1, source_target_pairs={{0,1},{1,2},{2,3},{3,4},{4,5},{5,6},{6,7},{7,8},{8,9},{9,10},{10,1... | collective-permute-start | bytes 1769480 | tf_op jit(solution)/shard_map/ppermute | solution.py:12
  31.7 13.2 %collective-permute-start.9 = (bf16[384]{0:T(512)(128)(2,1)S(1)}, bf16[384]{0:T(512)(128)(2,1)S(1)}, u32[]{:S(2)}, u32[]{:S(2)}) collective-permute-start(bf16[384]{0:T(512)(128)(2,1)S(1)} %get-tuple-element.141), channel_id=1, source_target_pairs={{0,62},{1,63},{2,0},{3,1},{4,2},{5,3},{6,4},{7,5},{8,6},{9,7},{10,... | collective-permute-start | bytes 2312 | tf_op jit(solution)/shard_map/ppermute | solution.py:12
  39.5 12.7 %collective-permute-start.4 = (bf16[384,768]{1,0:T(8,128)(2,1)S(1)}, bf16[384,768]{1,0:T(8,128)(2,1)S(1)}, u32[]{:S(2)}, u32[]{:S(2)}) collective-permute-start(bf16[384,768]{1,0:T(8,128)(2,1)S(1)} %fusion.38), channel_id=1, source_target_pairs={{0,63},{1,0},{2,1},{3,2},{4,3},{5,4},{6,5},{7,6},{8,7},{9,8},{10,9... | collective-permute-start | bytes 1769480 | tf_op jit(solution)/shard_map/ppermute | solution.py:12
  44.9 20.1 %collective-permute-start.7 = (bf16[384,768]{1,0:T(8,128)(2,1)S(1)}, bf16[384,768]{1,0:T(8,128)(2,1)S(1)}, u32[]{:S(2)}, u32[]{:S(2)}) collective-permute-start(bf16[384,768]{1,0:T(8,128)(2,1)S(1)} %fusion.38), channel_id=1, source_target_pairs={{0,2},{1,3},{2,4},{3,5},{4,6},{5,7},{6,8},{7,9},{8,10},{9,11},{10,... | collective-permute-start | bytes 1769480 | tf_op jit(solution)/shard_map/ppermute | solution.py:12
  46.8 18.2 %copy-start.9 = (bf16[384,768]{1,0:T(8,128)(2,1)}, bf16[384,768]{1,0:T(8,128)(2,1)S(1)}, u32[]{:S(2)}) copy-start(bf16[384,768]{1,0:T(8,128)(2,1)S(1)} %collective-permute-done.1) | copy-start | bytes 1769476
  46.9 62.8 %collective-permute-start.8 = (bf16[384,1024]{1,0:T(8,128)(2,1)S(1)}, bf16[384,1024]{1,0:T(8,128)(2,1)}, u32[]{:S(2)}, u32[]{:S(2)}) collective-permute-start(bf16[384,1024]{1,0:T(8,128)(2,1)S(1)} %fusion.36), channel_id=1, source_target_pairs={{0,2},{1,3},{2,4},{3,5},{4,6},{5,7},{6,8},{7,9},{8,10},{9,11},{10,... | collective-permute-start | bytes 2359304 | tf_op jit(solution)/shard_map/ppermute | solution.py:12
  52.2 12.9 %copy-start.7 = (bf16[384,768]{1,0:T(8,128)(2,1)}, bf16[384,768]{1,0:T(8,128)(2,1)S(1)}, u32[]{:S(2)}) copy-start(bf16[384,768]{1,0:T(8,128)(2,1)S(1)} %collective-permute-done.4) | copy-start | bytes 1769476
  52.2 76.8 %collective-permute-start.11 = (bf16[384,1024]{1,0:T(8,128)(2,1)S(1)}, bf16[384,1024]{1,0:T(8,128)(2,1)}, u32[]{:S(2)}, u32[]{:S(2)}) collective-permute-start(bf16[384,1024]{1,0:T(8,128)(2,1)S(1)} %fusion.36), channel_id=1, source_target_pairs={{0,62},{1,63},{2,0},{3,1},{4,2},{5,3},{6,4},{7,5},{8,6},{9,7},{10,... | collective-permute-start | bytes 2359304 | tf_op jit(solution)/shard_map/ppermute | solution.py:12
  65.0 0.8 copy-start.5
  65.9 71.1 %collective-permute-start.14 = (bf16[384,1024]{1,0:T(8,128)(2,1)S(1)}, bf16[384,1024]{1,0:T(8,128)(2,1)}, u32[]{:S(2)}, u32[]{:S(2)}) collective-permute-start(bf16[384,1024]{1,0:T(8,128)(2,1)S(1)} %fusion.36), channel_id=1, source_target_pairs={{0,64},{64,0},{128,192},{192,128},{256,320},{320,256},{384,448},{4... | collective-permute-start | bytes 2359304 | tf_op jit(solution)/shard_map/ppermute | solution.py:22
  68.1 60.8 %collective-permute-start.10 = (bf16[384,768]{1,0:T(8,128)(2,1)S(1)}, bf16[384,768]{1,0:T(8,128)(2,1)}, u32[]{:S(2)}, u32[]{:S(2)}) collective-permute-start(bf16[384,768]{1,0:T(8,128)(2,1)S(1)} %fusion.38), channel_id=1, source_target_pairs={{0,62},{1,63},{2,0},{3,1},{4,2},{5,3},{6,4},{7,5},{8,6},{9,7},{10,... | collective-permute-start | bytes 1769480 | tf_op jit(solution)/shard_map/ppermute | solution.py:12
  95.3 5.8 %copy-start.11 = (bf16[384,1024]{1,0:T(8,128)(2,1)}, bf16[384,1024]{1,0:T(8,128)(2,1)S(1)}, u32[]{:S(2)}) copy-start(bf16[384,1024]{1,0:T(8,128)(2,1)S(1)} %collective-permute-done.5) | copy-start | bytes 2359300
  95.3 41.6 %collective-permute-start.13 = (bf16[384,768]{1,0:T(8,128)(2,1)S(1)}, bf16[384,768]{1,0:T(8,128)(2,1)}, u32[]{:S(2)}, u32[]{:S(2)}) collective-permute-start(bf16[384,768]{1,0:T(8,128)(2,1)S(1)} %fusion.38), channel_id=1, source_target_pairs={{0,64},{64,0},{128,192},{192,128},{256,320},{320,256},{384,448},{4... | collective-permute-start | bytes 1769480 | tf_op jit(solution)/shard_map/ppermute | solution.py:22
  103.6 0.9 copy-start.12
  103.6 2.6 copy-start.10
  109.1 4.0 %copy-start.1 = (f32[384,768]{1,0:T(8,128)}, f32[384,768]{1,0:T(8,128)S(1)}, u32[]{:S(2)}) copy-start(f32[384,768]{1,0:T(8,128)S(1)} %get-tuple-element.107) | copy-start | bytes 3538948
  109.7 27.2 %collective-permute-start.12 = (bf16[384]{0:T(512)(128)(2,1)S(1)}, bf16[384]{0:T(512)(128)(2,1)S(1)}, u32[]{:S(2)}, u32[]{:S(2)}) collective-permute-start(bf16[384]{0:T(512)(128)(2,1)S(1)} %get-tuple-element.141), channel_id=1, source_target_pairs={{0,64},{64,0},{128,192},{192,128},{256,320},{320,256},{384,448},{4... | collective-permute-start | bytes 2312 | tf_op jit(solution)/shard_map/ppermute | solution.py:22
  113.1 1.8 copy-start.8
  119.0 1.8 copy-start.6
  123.8 5.2 %copy-start.2 = (f32[384,768]{1,0:T(8,128)}, f32[384,768]{1,0:T(8,128)S(1)}, u32[]{:S(2)}) copy-start(f32[384,768]{1,0:T(8,128)S(1)} %get-tuple-element.109) | copy-start | bytes 3538948
  137.1 1.0 copy-start.3
